TPU v7x, 32 devices: a whole 2x2x4 slice. The times are simulated.
32 devices in a mesh: dp: 8 (over z, y), expert: 4 (over x, core).
Axes of the slice: x: 2, y: 2, z: 4, core: 2. Of those that a mesh axis runs over, the one named last changes fastest.
Arguments:
- tokens: bfloat16 [4096, 2048], P(('dp', 'expert')), may hold values from -6 to 6
- routes: int32 [4096, 8], P(('dp', 'expert')), may hold values from 0 to 15, all different within a row; in each aligned block of 128 rows (0 to 127, 128 to 255, ...) at most 80 rows name the same one
- gates: bfloat16 [4096, 8], P(('dp', 'expert')), may hold values from 0.099609375 to 0.5
- cotangent: bfloat16 [4096, 2048], P(('dp', 'expert')), may hold values from -6 to 6
- w_gate: bfloat16 [16, 2048, 384], P('dp'), may hold values from -0.125 to 0.125
- w_up: bfloat16 [16, 2048, 384], P('dp'), may hold values from -0.125 to 0.125
- w_down: bfloat16 [16, 384, 2048], P('dp'), may hold values from -0.3125 to 0.3125
Outputs:
- layer_out: bfloat16 [4096, 2048], P(('dp', 'expert'))
- grad_tokens: bfloat16 [4096, 2048], P(('dp', 'expert'))
- grad_gate: bfloat16 [16, 2048, 384], P('dp', 'expert')
- grad_up: bfloat16 [16, 2048, 384], P('dp', 'expert')
- grad_down: bfloat16 [16, 384, 2048], P('dp', None, 'expert')
Inputs may be any that keep to these rules, and one draw needn't show every extreme that they name: `routes`: each row names 8 different experts. Among the rows of one device, no expert is named by more than 80 rows, and in every draw some device has an expert named by exactly 80 rows.
All inputs are finite; a program needn't handle non-finite values.
Results may differ from a plain program's by a relative error of at most 0.012.
Values may be sent and summed in bfloat16 or wider, within the bound.
A program may use at most 128 MiB of HBM per device.

v0:
```python
import jax
import jax.numpy as jnp
from jax import lax
from jax.sharding import PartitionSpec as P


def expert_forward(arrived, w_gate, w_up, w_down):
    gate_act = jnp.einsum("erd,edf->erf", arrived, w_gate, preferred_element_type=jnp.float32)
    up_act = jnp.einsum("erd,edf->erf", arrived, w_up, preferred_element_type=jnp.float32)
    sigma_gate = jax.nn.sigmoid(gate_act)
    smooth = gate_act * sigma_gate
    hidden = (smooth * up_act).astype(jnp.bfloat16)
    result = jnp.einsum("erf,efd->erd", hidden, w_down, preferred_element_type=jnp.float32).astype(
        jnp.bfloat16
    )
    return (gate_act, up_act, sigma_gate, smooth, hidden, result)


def body(tokens, routes, gates, cotangent, w_gate, w_up, w_down):
    tok_rows, top_k = routes.shape
    width = tokens.shape[1]
    owners = lax.axis_size("dp")
    per_owner = w_gate.shape[0]
    hidden_units = w_gate.shape[2]
    experts = owners * per_owner
    capacity = max(2, tok_rows * top_k * 5 // (4 * experts))
    slot_count = experts * capacity
    chosen = routes.reshape(-1)
    onehot = (chosen[:, None] == jnp.arange(experts, dtype=jnp.int32)[None, :]).astype(jnp.int32)
    order_in = jnp.sum((jnp.cumsum(onehot, axis=0) - onehot) * onehot, axis=1)
    slot_index = chosen * capacity + order_in
    token_of = jnp.arange(tok_rows * top_k, dtype=jnp.int32) // top_k
    table = jnp.full((slot_count,), tok_rows, jnp.int32).at[slot_index].set(token_of)
    slot_gain = (
        jnp.zeros((slot_count,), jnp.float32)
        .at[slot_index]
        .set(gates.reshape(-1).astype(jnp.float32))
    )
    padded_x = jnp.concatenate([tokens, jnp.zeros((1, width), tokens.dtype)], axis=0)
    padded_c = jnp.concatenate([cotangent, jnp.zeros((1, width), cotangent.dtype)], axis=0)
    send_rows = padded_x[table].reshape(experts, capacity, width)
    send_grads = (slot_gain[:, None] * padded_c[table].astype(jnp.float32)).astype(jnp.bfloat16)
    send_grads = send_grads.reshape(experts, capacity, width)
    arrived = lax.all_to_all(send_rows, "dp", split_axis=0, concat_axis=1, tiled=True)
    state = expert_forward(arrived, w_gate, w_up, w_down)
    arrived_grad = lax.all_to_all(send_grads, "dp", split_axis=0, concat_axis=1, tiled=True)
    gate_act, up_act, sigma_gate, smooth, hidden, result = state
    returned = lax.all_to_all(result, "dp", split_axis=1, concat_axis=0, tiled=True).reshape(
        slot_count, width
    )
    picked = returned[slot_index].reshape(tok_rows, top_k, width)
    layer_out = jnp.einsum("tk,tkd->td", gates, picked, preferred_element_type=jnp.float32).astype(
        jnp.bfloat16
    )
    grad_hidden = jnp.einsum(
        "erd,efd->erf", arrived_grad, w_down, preferred_element_type=jnp.float32
    )
    grad_upact = (grad_hidden * smooth).astype(jnp.bfloat16)
    grad_gateact = (
        grad_hidden * up_act * sigma_gate * (1.0 + gate_act * (1.0 - sigma_gate))
    ).astype(jnp.bfloat16)
    row_grads = (
        jnp.einsum("erf,edf->erd", grad_gateact, w_gate, preferred_element_type=jnp.float32)
        + jnp.einsum("erf,edf->erd", grad_upact, w_up, preferred_element_type=jnp.float32)
    ).astype(jnp.bfloat16)
    came_back = lax.all_to_all(row_grads, "dp", split_axis=1, concat_axis=0, tiled=True).reshape(
        slot_count, width
    )
    grad_picked = came_back[slot_index].reshape(tok_rows, top_k, width)
    grad_tokens = jnp.sum(grad_picked.astype(jnp.float32), axis=1).astype(jnp.bfloat16)
    both_factors = jnp.concatenate([grad_gateact, grad_upact], axis=2)
    input_term = jnp.einsum(
        "erd,erf->def", arrived, both_factors, preferred_element_type=jnp.float32
    )
    down_term = jnp.einsum("erf,erd->def", hidden, arrived_grad, preferred_element_type=jnp.float32)
    totals = lax.psum_scatter(
        jnp.concatenate([input_term, down_term], axis=2).astype(jnp.bfloat16),
        "expert",
        scatter_dimension=0,
        tiled=True,
    ).astype(jnp.float32)
    grad_gate = jnp.transpose(totals[:, :, :hidden_units], (1, 0, 2)).astype(jnp.bfloat16)
    grad_up = jnp.transpose(totals[:, :, hidden_units : 2 * hidden_units], (1, 0, 2)).astype(
        jnp.bfloat16
    )
    grad_down = jnp.transpose(totals[:, :, 2 * hidden_units :], (1, 2, 0)).astype(jnp.bfloat16)
    return (layer_out, grad_tokens, grad_gate, grad_up, grad_down)


def solution(mesh):
    return jax.shard_map(
        body,
        mesh=mesh,
        in_specs=(
            P(("dp", "expert"), None),
            P(("dp", "expert"), None),
            P(("dp", "expert"), None),
            P(("dp", "expert"), None),
            P("dp", None, None),
            P("dp", None, None),
            P("dp", None, None),
        ),
        out_specs=(
            P(("dp", "expert"), None),
            P(("dp", "expert"), None),
            P("dp", "expert", None),
            P("dp", "expert", None),
            P("dp", None, "expert"),
        ),
        check_vma=False,
    )
```

profile of v0, /device:TPU:0, one launch (start us, length us, event | category | flops | bytes accessed | tf_op | source)
XLA Modules:
  0.0 627.4 jit_solution(449941669003016595)
XLA Ops:
  9.0 4.5 reduce-window.6
  14.2 4.3 scatter_custom_fusion
  19.4 4.3 scatter_custom_fusion.1
  25.7 11.9 %gather_fusion.2 = bf16[1280,2048]{1,0:T(8,128)(2,1)} fusion(bf16[129,2048]{1,0:T(8,128)(2,1)} %concatenate.14, s32[2048]{0:T(1024)S(1)} %pad_clamp_fusion), kind=kCustom, calls=%fused_computation.2 | custom fusion | bytes 10490880 | tf_op jit(solution)/shard_map/gather | solution.py:42
  37.7 5.7 fusion
  43.4 7.3 %all-to-all-start.2 = ((bf16[16,80,2048]{2,1,0:T(8,128)(2,1)}), bf16[16,80,2048]{2,1,0:T(8,128)(2,1)}, u32[]{:S(2)}, u32[]{:S(2)}) async-start(bf16[16,80,2048]{2,1,0:T(8,128)(2,1)} %fusion), calls=%async_computation.2 | async-start | bytes 10485760 | tf_op jit(solution)/shard_map/all_to_all | solution.py:46
  52.6 12.0 %gather_fusion = bf16[1280,2048]{1,0:T(8,128)(2,1)} fusion(bf16[129,2048]{1,0:T(8,128)(2,1)} %concatenate.13, s32[2048]{0:T(1024)S(1)} %pad_clamp_fusion), kind=kCustom, calls=%fused_computation | custom fusion | bytes 10490880 | tf_op jit(solution)/shard_map/gather | solution.py:41
  64.5 101.9 %all-to-all-done.2 = bf16[16,80,2048]{2,1,0:T(8,128)(2,1)} async-done(((bf16[16,80,2048]{2,1,0:T(8,128)(2,1)}), bf16[16,80,2048]{2,1,0:T(8,128)(2,1)}, u32[]{:S(2)}, u32[]{:S(2)}) %all-to-all-start.2) | async-done | bytes 5242912 | tf_op jit(solution)/shard_map/all_to_all | solution.py:46
  166.4 4.8 all-to-all-start
  171.3 5.6 copy.52
  176.9 109.3 %all-to-all-done = bf16[16,80,2048]{2,1,0:T(8,128)(2,1)} async-done(((bf16[16,80,2048]{2,1,0:T(8,128)(2,1)}), bf16[16,80,2048]{2,1,0:T(8,128)(2,1)}, u32[]{:S(2)}, u32[]{:S(2)}) %all-to-all-start) | async-done | bytes 5242912 | tf_op jit(solution)/shard_map/all_to_all | solution.py:44
  289.6 4.2 fusion.20
  293.8 4.1 fusion.21
  297.9 6.0 multiply_convert_fusion
  303.9 3.1 fusion.22
  307.1 7.1 %convert_bitcast_fusion = bf16[2048,2,768]{0,2,1:T(8,128)(2,1)} fusion(bf16[2,640,2048]{2,1,0:T(8,128)(2,1)S(1)} %bitcast.86, bf16[2,640,384]{1,2,0:T(8,128)(2,1)S(1)} %copy-done.7, bf16[2,640,384]{1,2,0:T(8,128)(2,1)S(1)} %get-tuple-element.21), kind=kOutput, calls=%fused_computation.10 | convolution fusion | flops 4033609728 | bytes 13500416 | tf_op jit(solution)/shard_map/erd,erf->def/dot_general | solution.py:72
  314.3 4.0 fusion.3
  318.2 5.2 add_convert_fusion
  323.4 10.2 %copy.55 = bf16[2,640,2048]{2,0,1:T(2,128)(2,1)} copy(bf16[2,640,2048]{2,1,0:T(8,128)(2,1)} %add_convert_fusion) | data formatting | bytes 10485760 | tf_op jit(solution)/shard_map/convert_element_type | solution.py:65
  333.6 4.7 all-to-all-start.3
  338.4 8.2 %pad_maximum_fusion = bf16[2048,2,1152]{0,2,1:T(8,128)(2,1)} fusion(bf16[2048,2,384]{0,2,1:T(8,128)(2,1)} %fusion.3, bf16[2048,2,768]{0,2,1:T(8,128)(2,1)} %convert_bitcast_fusion), kind=kLoop, calls=%fused_computation.9 | loop fusion | flops 18874368 | bytes 18874368 | tf_op jit(solution)/shard_map/concatenate | solution.py:77
  346.6 5.9 convolution_convert_fusion
  352.6 11.0 %copy.49 = bf16[2,640,2048]{2,0,1:T(2,128)(2,1)} copy(bf16[2,640,2048]{2,1,0:T(8,128)(2,1)} %convolution_convert_fusion) | data formatting | bytes 10485760 | tf_op jit(solution)/shard_map/convert_element_type | solution.py:13
  363.6 89.6 %all-to-all-done.3 = bf16[2,640,2048]{2,0,1:T(2,128)(2,1)} async-done(((bf16[2,640,2048]{2,0,1:T(2,128)(2,1)}), bf16[2,640,2048]{2,0,1:T(2,128)(2,1)}, u32[]{:S(2)}, u32[]{:S(2)}) %all-to-all-start.3) | async-done | bytes 5242912 | tf_op jit(solution)/shard_map/all_to_all | solution.py:66
  453.2 4.8 all-to-all-start.1
  458.2 7.2 %copy.56 = bf16[2,8,80,2048]{3,2,0,1:T(8,128)(2,1)} copy(bf16[2,8,80,2048]{3,0,2,1:T(2,128)(2,1)} %bitcast.18) | data formatting | bytes 10485760 | tf_op jit(solution)/shard_map/all_to_all | solution.py:66
  465.4 107.5 %all-to-all-done.1 = bf16[2,640,2048]{2,0,1:T(2,128)(2,1)} async-done(((bf16[2,640,2048]{2,0,1:T(2,128)(2,1)}), bf16[2,640,2048]{2,0,1:T(2,128)(2,1)}, u32[]{:S(2)}, u32[]{:S(2)}) %all-to-all-start.1) | async-done | bytes 5242912 | tf_op jit(solution)/shard_map/all_to_all | solution.py:48
  572.9 7.3 %copy.50 = bf16[2,8,80,2048]{3,2,0,1:T(8,128)(2,1)} copy(bf16[2,8,80,2048]{3,0,2,1:T(2,128)(2,1)} %bitcast.8) | data formatting | bytes 10485760 | tf_op jit(solution)/shard_map/all_to_all | solution.py:48
  580.2 12.0 %gather_fusion.3 = bf16[1024,2048]{1,0:T(8,128)(2,1)} fusion(bf16[1280,2048]{1,0:T(8,128)(2,1)} %bitcast.74, s32[1024]{0:T(1024)S(1)} %broadcast_clamp_fusion), kind=kCustom, calls=%fused_computation.3 | custom fusion | bytes 8392704 | tf_op jit(solution)/shard_map/gather | solution.py:69
  592.2 12.2 %gather_fusion.1 = bf16[1024,2048]{1,0:T(8,128)(2,1)} fusion(bf16[1280,2048]{1,0:T(8,128)(2,1)} %bitcast.75, s32[1024]{0:T(1024)S(1)} %broadcast_clamp_fusion), kind=kCustom, calls=%fused_computation.1 | custom fusion | bytes 8392704 | tf_op jit(solution)/shard_map/gather | solution.py:51
  604.3 3.6 fusion.1
  609.0 3.7 bitcast_reduce_fusion
  (65 shorter events, 19.6 us)
Async XLA Ops:
  7.2 290.7 %copy-start = (bf16[2,384,2048]{2,1,0:T(8,128)(2,1)S(1)}, bf16[2,384,2048]{2,1,0:T(8,128)(2,1)}, u32[]{:S(2)}) copy-start(bf16[2,384,2048]{2,1,0:T(8,128)(2,1)} %param.13) | copy-start | bytes 9437188
  43.4 123.1 %all-to-all-start.2 = ((bf16[16,80,2048]{2,1,0:T(8,128)(2,1)}), bf16[16,80,2048]{2,1,0:T(8,128)(2,1)}, u32[]{:S(2)}, u32[]{:S(2)}) async-start(bf16[16,80,2048]{2,1,0:T(8,128)(2,1)} %fusion), calls=%async_computation.2 | async-start | bytes 10485760 | tf_op jit(solution)/shard_map/all_to_all | solution.py:46
  166.4 119.7 %all-to-all-start = ((bf16[16,80,2048]{2,1,0:T(8,128)(2,1)}), bf16[16,80,2048]{2,1,0:T(8,128)(2,1)}, u32[]{:S(2)}, u32[]{:S(2)}) async-start(bf16[16,80,2048]{2,1,0:T(8,128)(2,1)} %bitcast.76), calls=%async_computation | async-start | bytes 10485760 | tf_op jit(solution)/shard_map/all_to_all | solution.py:44
  286.2 3.4 copy-start.4
  289.3 4.5 copy-start.2
  289.6 4.2 copy-start.5
  289.6 8.3 %slice-start = ((s8[5242880]{0:T(1024)(128)(4,1)}), s8[4194304]{0:T(1024)(128)(4,1)S(1)}, s32[]{:S(2)}) async-start(s8[5242880]{0:T(1024)(128)(4,1)} %bitcast.78), calls=%async_computation.6 | async-start | bytes 8388608
  293.8 4.1 slice-start.1
  303.9 3.2 copy-start.3
  303.9 3.2 copy-start.7
  303.9 10.3 %slice-start.2 = ((s8[5242880]{0:T(1024)(128)(4,1)}), s8[4194304]{0:T(1024)(128)(4,1)S(1)}, s32[]{:S(2)}) async-start(s8[5242880]{0:T(1024)(128)(4,1)} %bitcast.81), calls=%async_computation.8 | async-start | bytes 8388608
  307.1 7.2 %slice-start.3 = ((s8[5242880]{0:T(1024)(128)(4,1)}), s8[1048576]{0:T(1024)(128)(4,1)S(1)}, s32[]{:S(2)}) async-start(s8[5242880]{0:T(1024)(128)(4,1)} %bitcast.81), calls=%async_computation.9 | async-start | bytes 2097152
  307.1 7.1 %copy-start.10 = (bf16[2,640,384]{1,2,0:T(8,128)(2,1)S(1)}, bf16[2,640,384]{1,2,0:T(8,128)(2,1)}, u32[]{:S(2)}) copy-start(bf16[2,640,384]{1,2,0:T(8,128)(2,1)} %get-tuple-element.22) | copy-start | bytes 2949124
  314.2 4.0 copy-start.6
  314.2 4.0 copy-start.8
  333.6 119.6 %all-to-all-start.3 = ((bf16[2,640,2048]{2,0,1:T(2,128)(2,1)}), bf16[2,640,2048]{2,0,1:T(2,128)(2,1)}, u32[]{:S(2)}, u32[]{:S(2)}) async-start(bf16[2,640,2048]{2,0,1:T(2,128)(2,1)} %copy.55), calls=%async_computation.3 | async-start | bytes 10485760 | tf_op jit(solution)/shard_map/all_to_all | solution.py:66
  338.4 274.3 %reduce-scatter.2.cloned.1.call-start = ((), (), s32[]{:S(2)}) async-start(), calls=%async_computation.5 | async-start | bytes 11796480 | tf_op jit(solution)/shard_map/reduce_scatter | solution.py:76
  363.6 94.4 %copy-start.9 = (bf16[128,8]{0,1:T(8,128)(2,1)S(1)}, bf16[128,8]{0,1:T(8,128)(2,1)}, u32[]{:S(2)}) copy-start(bf16[128,8]{0,1:T(8,128)(2,1)} %param.9) | copy-start | bytes 6148
  453.2 119.7 %all-to-all-start.1 = ((bf16[2,640,2048]{2,0,1:T(2,128)(2,1)}), bf16[2,640,2048]{2,0,1:T(2,128)(2,1)}, u32[]{:S(2)}, u32[]{:S(2)}) async-start(bf16[2,640,2048]{2,0,1:T(2,128)(2,1)} %copy.49), calls=%async_computation.1 | async-start | bytes 10485760 | tf_op jit(solution)/shard_map/all_to_all | solution.py:48
  604.3 4.7 copy-start.1
Sparse Core Ops, SparseCore 0:
  346.8 79.0 reduce-scatter.1
where the time goes:
time: 635 us; the launch traced here: 627 us
  waiting for transfers between devices  408 us (64%)
  local copies, waits for them, and re-layouts  117 us (18%)
  matrix products  43.2 us (7%)
  other arithmetic  23 us (4%)
  starting transfers between devices  21.7 us (3%)
  between operations  14.5 us (2%)
    all_to_all x1, waiting for transfers between devices, body(): lax.all_to_all(send_rows, 'dp', split_axis=0, concat_axis=1, tiled=True)  109 us
    all_to_all x1, waiting for transfers between devices, body(): lax.all_to_all(result, 'dp', split_axis=1, concat_axis=0, tiled=True)  108 us
    all_to_all x1, waiting for transfers between devices, body(): lax.all_to_all(send_grads, 'dp', split_axis=0, concat_axis=1, tiled=True)  102 us
    all_to_all x1, waiting for transfers between devices, body(): lax.all_to_all(row_grads, 'dp', split_axis=1, concat_axis=0, tiled=True)  89.6 us
  transfers between devices with their start and end apart: 5, of which 4 were waited for; matrix products, arithmetic and copies ran while one was open for 15% of the time, Pallas kernels for 0%

commit v1 on v0

--- a/solution.py
+++ b/solution.py
@@ -63,9 +63,10 @@
         jnp.einsum("erf,edf->erd", grad_gateact, w_gate, preferred_element_type=jnp.float32)
         + jnp.einsum("erf,edf->erd", grad_upact, w_up, preferred_element_type=jnp.float32)
     ).astype(jnp.bfloat16)
-    came_back = lax.all_to_all(row_grads, "dp", split_axis=1, concat_axis=0, tiled=True).reshape(
-        slot_count, width
-    )
+    came_back = jnp.concatenate(
+        lax.all_to_all(jnp.stack(jnp.split(row_grads, lax.axis_size("dp"), axis=1)), "dp", 0, 0),
+        axis=0,
+    ).reshape(slot_count, width)
     grad_picked = came_back[slot_index].reshape(tok_rows, top_k, width)
     grad_tokens = jnp.sum(grad_picked.astype(jnp.float32), axis=1).astype(jnp.bfloat16)
     both_factors = jnp.concatenate([grad_gateact, grad_upact], axis=2)

time: 635 us -> 614 us (0.967)
  waiting for transfers between devices: 408 us -> 389 us
    all_to_all x1, waiting for transfers between devices: 108 us -> 70.2 us  [body(): lax.all_to_all(result, 'dp', split_axis=1, concat_axis=0, tiled=True)]
    all_to_all x1, waiting for transfers between devices: 89.6 us -> 108 us  [body(): lax.all_to_all(jnp.stack(jnp.split(row_grads, lax.axis_size('dp'), axis=1...]
    unnamed x34 -> x37, local copies, waits for them, and re-layouts: 6.04 us -> 23 us
    convert_element_type x1 -> x0, local copies, waits for them, and re-layouts: 10.2 us -> none  [body(): row_grads = (jnp.einsum('erf,edf->erd', grad_gateact, w_gate, preferred_e...]
    all_to_all x1 -> x0, local copies, waits for them, and re-layouts: 7.24 us -> none  [body(): lax.all_to_all(row_grads, 'dp', split_axis=1, concat_axis=0, tiled=True)]
  transfers between devices with their start and end apart: 5 -> 5, of which waited for: 4 -> 4; matrix products, arithmetic and copies ran while one was open for 15% -> 17% of each run, Pallas kernels for 0% -> 0%
where the time goes in v1:
time: 614 us; the launch traced here: 607 us
  waiting for transfers between devices  389 us (63%)
  local copies, waits for them, and re-layouts  117 us (19%)
  matrix products  40.5 us (7%)
  other arithmetic  23.3 us (4%)
  starting transfers between devices  22 us (4%)
  between operations  14.5 us (2%)
    all_to_all x1, waiting for transfers between devices, body(): lax.all_to_all(send_rows, 'dp', split_axis=0, concat_axis=1, tiled=True)  109 us
    all_to_all x1, waiting for transfers between devices, body(): lax.all_to_all(jnp.stack(jnp.split(row_grads, lax.axis_size('dp'), axis=1...  108 us
    all_to_all x1, waiting for transfers between devices, body(): lax.all_to_all(send_grads, 'dp', split_axis=0, concat_axis=1, tiled=True)  102 us
    all_to_all x1, waiting for transfers between devices, body(): lax.all_to_all(result, 'dp', split_axis=1, concat_axis=0, tiled=True)  70.2 us
    unnamed x37, local copies, waits for them, and re-layouts  23 us
  transfers between devices with their start and end apart: 5, of which 4 were waited for; matrix products, arithmetic and copies ran while one was open for 17% of the time, Pallas kernels for 0%

profile of v1, /device:TPU:0, one launch (start us, length us, event | category | flops | bytes accessed | tf_op | source)
XLA Modules:
  0.0 606.6 jit_solution(9786638141905217063)
XLA Ops:
  9.0 4.5 reduce-window.6
  14.2 4.3 scatter_custom_fusion
  19.4 4.3 scatter_custom_fusion.1
  25.7 11.9 %gather_fusion.2 = bf16[1280,2048]{1,0:T(8,128)(2,1)} fusion(bf16[129,2048]{1,0:T(8,128)(2,1)} %concatenate.14, s32[2048]{0:T(1024)S(1)} %pad_clamp_fusion), kind=kCustom, calls=%fused_computation.2 | custom fusion | bytes 10490880 | tf_op jit(solution)/shard_map/gather | solution.py:42
  37.7 5.8 fusion
  43.4 7.3 %all-to-all-start.2 = ((bf16[16,80,2048]{2,1,0:T(8,128)(2,1)}), bf16[16,80,2048]{2,1,0:T(8,128)(2,1)}, u32[]{:S(2)}, u32[]{:S(2)}) async-start(bf16[16,80,2048]{2,1,0:T(8,128)(2,1)} %fusion), calls=%async_computation.2 | async-start | bytes 10485760 | tf_op jit(solution)/shard_map/all_to_all | solution.py:46
  52.6 11.9 %gather_fusion = bf16[1280,2048]{1,0:T(8,128)(2,1)} fusion(bf16[129,2048]{1,0:T(8,128)(2,1)} %concatenate.13, s32[2048]{0:T(1024)S(1)} %pad_clamp_fusion), kind=kCustom, calls=%fused_computation | custom fusion | bytes 10490880 | tf_op jit(solution)/shard_map/gather | solution.py:41
  64.6 101.9 %all-to-all-done.2 = bf16[16,80,2048]{2,1,0:T(8,128)(2,1)} async-done(((bf16[16,80,2048]{2,1,0:T(8,128)(2,1)}), bf16[16,80,2048]{2,1,0:T(8,128)(2,1)}, u32[]{:S(2)}, u32[]{:S(2)}) %all-to-all-start.2) | async-done | bytes 5242912 | tf_op jit(solution)/shard_map/all_to_all | solution.py:46
  166.5 5.1 all-to-all-start
  171.6 5.7 copy.50
  177.3 109.2 %all-to-all-done = bf16[16,80,2048]{2,1,0:T(8,128)(2,1)} async-done(((bf16[16,80,2048]{2,1,0:T(8,128)(2,1)}), bf16[16,80,2048]{2,1,0:T(8,128)(2,1)}, u32[]{:S(2)}, u32[]{:S(2)}) %all-to-all-start) | async-done | bytes 5242912 | tf_op jit(solution)/shard_map/all_to_all | solution.py:44
  286.5 3.3 copy.43
  290.0 2.9 fusion.28
  293.6 2.9 fusion.29
  296.5 4.7 multiply_convert_fusion
  301.2 3.9 fusion.3
  305.2 4.9 convolution_convert_fusion
  310.1 10.1 %copy.47 = bf16[2,640,2048]{2,0,1:T(2,128)(2,1)} copy(bf16[2,640,2048]{2,1,0:T(8,128)(2,1)} %convolution_convert_fusion) | data formatting | bytes 10485760 | tf_op jit(solution)/shard_map/convert_element_type | solution.py:13
  320.2 4.7 all-to-all-start.1
  324.9 7.7 %convert_bitcast_fusion = bf16[2048,2,768]{0,2,1:T(8,128)(2,1)S(1)} fusion(bf16[2,640,2048]{2,1,0:T(8,128)(2,1)} %bitcast.108, bf16[2,640,384]{1,2,0:T(8,128)(2,1)} %get-tuple-element.20, bf16[2,640,384]{1,2,0:T(8,128)(2,1)} %get-tuple-element.21), kind=kOutput, calls=%fused_computation.10 | convolution fusion | flops 4033609728 | bytes 13500416 | tf_op jit(solution)/shard_map/erd,erf->def/dot_general | solution.py:73
  332.7 8.5 %pad_maximum_fusion = bf16[2048,2,1152]{0,2,1:T(8,128)(2,1)} fusion(bf16[2048,2,384]{0,2,1:T(8,128)(2,1)S(1)} %copy-done.8, bf16[2048,2,768]{0,2,1:T(8,128)(2,1)S(1)} %convert_bitcast_fusion), kind=kLoop, calls=%fused_computation.9 | loop fusion | flops 18874368 | bytes 18874368 | tf_op jit(solution)/shard_map/concatenate | solution.py:78
  343.1 4.4 fusion.30
  347.5 5.5 add_convert_fusion
  369.6 70.2 %all-to-all-done.1 = bf16[2,640,2048]{2,0,1:T(2,128)(2,1)} async-done(((bf16[2,640,2048]{2,0,1:T(2,128)(2,1)}), bf16[2,640,2048]{2,0,1:T(2,128)(2,1)}, u32[]{:S(2)}, u32[]{:S(2)}) %all-to-all-start.1) | async-done | bytes 5242912 | tf_op jit(solution)/shard_map/all_to_all | solution.py:48
  439.8 4.9 all-to-all-start.3
  444.8 7.2 %copy.48 = bf16[2,8,80,2048]{3,2,0,1:T(8,128)(2,1)} copy(bf16[2,8,80,2048]{3,0,2,1:T(2,128)(2,1)} %bitcast.8) | data formatting | bytes 10485760 | tf_op jit(solution)/shard_map/all_to_all | solution.py:48
  451.9 107.6 %all-to-all-done.3 = bf16[8,2,80,2048]{3,2,1,0:T(8,128)(2,1)} async-done(((bf16[8,2,80,2048]{3,2,1,0:T(8,128)(2,1)}), bf16[8,2,80,2048]{3,2,1,0:T(8,128)(2,1)}, u32[]{:S(2)}, u32[]{:S(2)}) %all-to-all-start.3) | async-done | bytes 5242912 | tf_op jit(solution)/shard_map/all_to_all | solution.py:67
  559.5 12.0 %gather_fusion.3 = bf16[1024,2048]{1,0:T(8,128)(2,1)} fusion(bf16[1280,2048]{1,0:T(8,128)(2,1)} %bitcast.26, s32[1024]{0:T(1024)S(1)} %broadcast_clamp_fusion), kind=kCustom, calls=%fused_computation.3 | custom fusion | bytes 8392704 | tf_op jit(solution)/shard_map/gather | solution.py:70
  571.5 12.0 %gather_fusion.1 = bf16[1024,2048]{1,0:T(8,128)(2,1)} fusion(bf16[1280,2048]{1,0:T(8,128)(2,1)} %bitcast.103, s32[1024]{0:T(1024)S(1)} %broadcast_clamp_fusion), kind=kCustom, calls=%fused_computation.1 | custom fusion | bytes 8392704 | tf_op jit(solution)/shard_map/gather | solution.py:51
  583.5 3.6 fusion.1
  588.2 3.7 bitcast_reduce_fusion
  591.9 3.1 slice_bitcast_fusion
  (66 shorter events, 32.4 us)
Async XLA Ops:
  7.2 289.3 %copy-start = (bf16[2,384,2048]{2,1,0:T(8,128)(2,1)S(1)}, bf16[2,384,2048]{2,1,0:T(8,128)(2,1)}, u32[]{:S(2)}) copy-start(bf16[2,384,2048]{2,1,0:T(8,128)(2,1)} %param.13) | copy-start | bytes 9437188
  43.4 123.1 %all-to-all-start.2 = ((bf16[16,80,2048]{2,1,0:T(8,128)(2,1)}), bf16[16,80,2048]{2,1,0:T(8,128)(2,1)}, u32[]{:S(2)}, u32[]{:S(2)}) async-start(bf16[16,80,2048]{2,1,0:T(8,128)(2,1)} %fusion), calls=%async_computation.2 | async-start | bytes 10485760 | tf_op jit(solution)/shard_map/all_to_all | solution.py:46
  166.5 120.0 %all-to-all-start = ((bf16[16,80,2048]{2,1,0:T(8,128)(2,1)}), bf16[16,80,2048]{2,1,0:T(8,128)(2,1)}, u32[]{:S(2)}, u32[]{:S(2)}) async-start(bf16[16,80,2048]{2,1,0:T(8,128)(2,1)} %bitcast.104), calls=%async_computation | async-start | bytes 10485760 | tf_op jit(solution)/shard_map/all_to_all | solution.py:44
  286.5 3.4 copy-start.4
  289.8 3.1 copy-start.3
  290.0 3.6 copy-start.6
  290.0 6.5 %slice-start = ((s8[5242880]{0:T(1024)(128)(4,1)}), s8[4194304]{0:T(1024)(128)(4,1)S(1)}, s32[]{:S(2)}) async-start(s8[5242880]{0:T(1024)(128)(4,1)} %bitcast.109), calls=%async_computation.6 | async-start | bytes 8388608
  293.6 2.9 slice-start.1
  320.2 119.6 %all-to-all-start.1 = ((bf16[2,640,2048]{2,0,1:T(2,128)(2,1)}), bf16[2,640,2048]{2,0,1:T(2,128)(2,1)}, u32[]{:S(2)}, u32[]{:S(2)}) async-start(bf16[2,640,2048]{2,0,1:T(2,128)(2,1)} %copy.47), calls=%async_computation.1 | async-start | bytes 10485760 | tf_op jit(solution)/shard_map/all_to_all | solution.py:48
  324.9 267.0 %reduce-scatter.2.cloned.1.call-start = ((), (), s32[]{:S(2)}) async-start(), calls=%async_computation.5 | async-start | bytes 11796480 | tf_op jit(solution)/shard_map/reduce_scatter | solution.py:77
  324.9 7.8 %copy-start.8 = (bf16[2048,2,384]{0,2,1:T(8,128)(2,1)S(1)}, bf16[2048,2,384]{0,2,1:T(8,128)(2,1)}, u32[]{:S(2)}) copy-start(bf16[2048,2,384]{0,2,1:T(8,128)(2,1)} %fusion.3) | copy-start | bytes 9437188
  341.2 1.9 copy-start.5
  343.1 4.4 copy-start.7
  343.1 4.4 copy-start.9
  369.5 75.1 %copy-start.10 = (bf16[128,8]{0,1:T(8,128)(2,1)S(1)}, bf16[128,8]{0,1:T(8,128)(2,1)}, u32[]{:S(2)}) copy-start(bf16[128,8]{0,1:T(8,128)(2,1)} %param.9) | copy-start | bytes 6148
  439.8 119.8 %all-to-all-start.3 = ((bf16[8,2,80,2048]{3,2,1,0:T(8,128)(2,1)}), bf16[8,2,80,2048]{3,2,1,0:T(8,128)(2,1)}, u32[]{:S(2)}, u32[]{:S(2)}) async-start(bf16[8,2,80,2048]{3,2,1,0:T(8,128)(2,1)} %fusion.8), calls=%async_computation.3 | async-start | bytes 10485760 | tf_op jit(solution)/shard_map/all_to_all | solution.py:67
  583.5 4.7 copy-start.2
  587.1 12.4 %copy-start.1 = (bf16[2,384,2048]{2,1,0:T(8,128)(2,1)S(1)}, bf16[2,384,2048]{2,1,0:T(8,128)(2,1)}, u32[]{:S(2)}) copy-start(bf16[2,384,2048]{2,1,0:T(8,128)(2,1)} %param.13) | copy-start | bytes 9437188
Sparse Core Ops, SparseCore 0:
  341.3 79.0 reduce-scatter.1
